TPU v7x, 256 devices: a whole 4x4x8 slice. The times are simulated.
256 devices in a mesh: space: 32 (over z, x), tm: 8 (over y, core).
Axes of the slice: x: 4, y: 4, z: 8, core: 2. Of those that a mesh axis runs over, the one named last changes fastest.
Arguments:
- iterate: float32 [8, 240, 23040], P(None, 'tm', 'space'), may hold values from -6 to 6
- residual: float32 [8, 240, 23040], P(None, 'tm', 'space'), may hold values from -24 to 24
- direction: float32 [8, 240, 23040], P(None, 'tm', 'space'), may hold values from -24 to 24
- diffusivity: float32 [23040], P('space'), may hold values from 0.1 to 0.34
- temporal_factor: float32 [240, 240], replicated, may hold values from 0 to 4
- block_tile: int32 [8, 256], P('tm', 'space'), may hold values from -1 to 479, as said below
- footprints: bfloat16 [8, 256, 64, 1440], P('tm', 'space'), may hold values from -0.15625 to 0.15625
- obs_weight: float32 [8, 32, 64], P('tm', 'space'), may hold values from 0.3 to 3
Outputs:
- iterate_next: float32 [8, 240, 23040], P(None, 'tm', 'space')
- residual_next: float32 [8, 240, 23040], P(None, 'tm', 'space')
- direction_next: float32 [8, 240, 23040], P(None, 'tm', 'space')
Inputs may be any that keep to these rules, and one draw needn't show every extreme that they name: `block_tile`: entry -1 marks a padding slot. Tile g belongs to index g // 15 of space. The valid entries of one device name distinct tiles, at most 2 of them of one owner; in each row of tm one owner is named exactly 2 times by every device.
All inputs are finite; a program needn't handle non-finite values.
Results may differ from a plain program's by a relative error of at most 0.017.
Values may be sent and summed in bfloat16 or wider, within the bound.
No kernel may reach another device: no remote copies, remote signals or barrier semaphores. Data moves between devices by JAX's collectives and lax.ppermute only.
A program may use at most 128 MiB of HBM per device.

v0:
```python
import jax
import jax.numpy as jnp
from jax import lax
from jax.sharding import PartitionSpec as P

LON = 720
TC = 48
NB = 8
DIFF = 2


def for_sending(value):

    def short(part):
        return part.astype(jnp.bfloat16) if part.dtype == jnp.float32 else part

    return jax.tree.map(short, value)


def extended_2(cells, sides, width):
    for axis, dim in sides:
        count = lax.axis_size(axis)
        ends = count - 1
        head = lax.slice_in_dim(cells, 0, width, axis=dim)
        tail = lax.slice_in_dim(cells, cells.shape[dim] - width, cells.shape[dim], axis=dim)
        cells = jnp.concatenate(
            [
                lax.ppermute(tail, axis, [(i, (i + 1) % count) for i in range(ends)]),
                cells,
                lax.ppermute(head, axis, [((i + 1) % count, i) for i in range(ends)]),
            ],
            axis=dim,
        )
    return cells


def temporal(field, matrix):
    combined = jnp.einsum(
        "tu,kuc->ktc",
        matrix,
        lax.all_to_all(
            field.astype(jnp.bfloat16), "tm", split_axis=2, concat_axis=1, tiled=True
        ).astype(field.dtype),
        precision=lax.Precision.HIGHEST,
    )
    return lax.all_to_all(
        for_sending(combined), "tm", split_axis=1, concat_axis=2, tiled=True
    ).astype(combined.dtype)


def diffuse(field, conduct):
    samples, window, cell_count = field.shape
    rows_here = cell_count // LON
    for sweep_index in range(DIFF):
        scaled_field = field * conduct
        extended = extended_2(for_sending(scaled_field), (("space", 2),), LON).astype(
            scaled_field.dtype
        )
        planes = extended.reshape(samples, window, rows_here + 2, LON)
        centre = planes[:, :, 1:-1, :]
        laplace = (
            planes[:, :, :-2, :]
            + planes[:, :, 2:, :]
            + jnp.roll(centre, 1, 3)
            + jnp.roll(centre, -1, 3)
            - 4.0 * centre
        )
        field = field + conduct * laplace.reshape(samples, window, cell_count)
    return field


def local(
    iterate, residual, direction, diffusivity, temporal_factor, block_tile, footprints, obs_weight
):
    samples, window, cell_count = direction.shape
    tiles_here = cell_count // TC
    entries = block_tile[0]
    blocks_here = entries.shape[0]
    present = entries >= 0
    mixed = temporal(direction, temporal_factor)
    spread = diffuse(mixed, diffusivity)
    tiled = spread.astype(jnp.bfloat16).reshape(samples, window, tiles_here, TC)
    empty_blocks = jnp.zeros((blocks_here, samples, window * TC), jnp.float32)
    segment = lax.all_gather(tiled, "space", axis=2, tiled=True)
    count_tiles = segment.shape[2]
    selector = (entries[:, None] == jnp.arange(count_tiles)[None, :]).astype(jnp.bfloat16)
    picked = jnp.einsum("bj,ktjc->bktc", selector, segment, preferred_element_type=jnp.float32)
    blocks = picked.reshape(empty_blocks.shape).astype(jnp.bfloat16)
    footprint = footprints[0]
    batches = obs_weight.shape[1]
    slot_obs = jnp.einsum("bmx,bkx->bkm", footprint, blocks, preferred_element_type=jnp.float32)
    batch_obs = jnp.sum(slot_obs.reshape(batches, NB, samples, footprint.shape[1]), axis=1)
    weighted = (obs_weight[0][:, None, :] * batch_obs).astype(jnp.bfloat16)
    grouped = footprint.reshape(batches, NB, footprint.shape[1], footprint.shape[2])
    gradient = jnp.einsum("anmx,akm->ankx", grouped, weighted, preferred_element_type=jnp.float32)
    gradient = gradient.reshape(blocks_here, samples, footprint.shape[2])
    gradient = jnp.where(present[:, None, None], gradient, 0.0).astype(jnp.bfloat16)
    selector = (
        entries[:, None] == jnp.arange(lax.axis_size("space") * tiles_here)[None, :]
    ).astype(jnp.bfloat16)
    summed = lax.psum_scatter(
        jnp.einsum("bj,bkx->jkx", selector, gradient, preferred_element_type=jnp.float32).astype(
            jnp.bfloat16
        ),
        "space",
        scatter_dimension=0,
        tiled=True,
    ).astype(jnp.float32)
    pulled = (
        summed.reshape(tiles_here, samples, window, TC)
        .transpose(1, 2, 0, 3)
        .reshape(samples, window, cell_count)
    )
    back = diffuse(pulled, diffusivity)
    image = direction + temporal(back, temporal_factor.T)
    old_norm, curvature = lax.psum(
        (jnp.sum(residual * residual, axis=(1, 2)), jnp.sum(direction * image, axis=(1, 2))),
        ("space", "tm"),
    )
    step_size = old_norm / curvature
    residual_next = residual - step_size[:, None, None] * image
    new_norm = lax.psum(jnp.sum(residual_next * residual_next, axis=(1, 2)), ("space", "tm"))
    iterate_next = iterate + step_size[:, None, None] * direction
    direction_next = residual_next + (new_norm / old_norm)[:, None, None] * direction
    return (iterate_next, residual_next, direction_next)


def solution(mesh):
    return jax.shard_map(
        local,
        mesh=mesh,
        in_specs=(
            P(None, "tm", "space"),
            P(None, "tm", "space"),
            P(None, "tm", "space"),
            P("space"),
            P(),
            P("tm", "space"),
            P("tm", "space", None, None),
            P("tm", "space", None),
        ),
        out_specs=(P(None, "tm", "space"), P(None, "tm", "space"), P(None, "tm", "space")),
        check_vma=False,
    )
```

profile of v0, /device:TPU:1, one launch (start us, length us, event | category | flops | bytes accessed | tf_op | source)
XLA Modules:
  0.0 833.4 jit_solution(11026537258770947451)
XLA Ops:
  7.2 1.3 convert_element_type.141
  8.5 1.5 copy.95
  10.0 2.0 reshape.151
  12.0 14.0 %all_to_all.54 = bf16[8,2,10800]{2,1,0:T(2,128)(2,1)} all-to-all(bf16[8,2,10800]{2,1,0:T(2,128)(2,1)S(1)} %reshape.151), channel_id=1, replica_groups=mesh['space'=32,'tm'=8] {'tm'}, dimensions={0} | all-to-all | bytes 691200 | tf_op jit(solution)/shard_map/all_to_all | solution.py:41
  26.0 3.1 reshape.152
  30.2 1.6 fusion.12
  32.1 12.3 %all_to_all.55 = bf16[8,240,90]{2,0,1:T(8,128)(2,1)S(1)} all-to-all(bf16[8,240,90]{2,0,1:T(8,128)(2,1)S(1)} %copy.98), channel_id=1, replica_groups=mesh['space'=32,'tm'=8] {'tm'}, dimensions={1} | all-to-all | bytes 691200 | tf_op jit(solution)/shard_map/all_to_all | solution.py:46
  46.0 1.9 multiply_convert_fusion.6
  47.9 3.4 collective-permute-start
  51.3 1.3 collective-permute-start.1
  54.9 2.8 collective-permute-done
  57.7 4.6 collective-permute-done.1
  62.3 1.3 maximum_convert_fusion
  67.5 3.1 collective-permute-start.2
  70.7 1.5 collective-permute-start.3
  72.2 1.3 copy.99
  73.5 2.7 reshape.137
  76.2 3.1 reshape.128
  81.4 1.4 maximum_convert_fusion.1
  83.1 1.2 fusion.38
  84.3 3.1 reshape.130
  87.4 4.9 fusion.5
  93.8 215.8 %all-gather.2.cloned.1.call-done = bf16[8,30,480,48]{3,0,1,2:T(8,128)(2,1)} async-done(((bf16[8,30,15,48]{3,0,1,2:T(8,128)(2,1)}), bf16[8,30,480,48]{3,0,1,2:T(8,128)(2,1)}) %all-gather.2.cloned.1.call-update) | async-done | bytes 11059216 | tf_op jit(solution)/shard_map/all_gather | solution.py:84
  309.6 26.4 %fusion.9 = bf16[8,8,30,48]{3,0,2,1:T(8,128)(2,1)S(1)} fusion(bf16[8,30,480,48]{3,0,1,2:T(8,128)(2,1)} %all-gather.2.cloned.1.call-done, s32[8]{0:T(128)S(1)} %bitcast.153), kind=kOutput, calls=%fused_computation.14 | convolution fusion | flops 88569600 | bytes 11243552 | tf_op jit(solution)/shard_map/bj,ktjc->bktc/dot_general | solution.py:87
  336.9 1.2 fusion.3
  338.1 3.7 convolution_convert_fusion
  341.8 20.4 %copy.109 = bf16[480,8,1440]{2,1,0:T(8,128)(2,1)} copy(bf16[480,8,1440]{2,0,1:T(8,128)(2,1)S(1)} %convolution_convert_fusion) | data formatting | bytes 22118400 | tf_op jit(solution)/shard_map/convert_element_type | solution.py:102
  362.2 230.0 %reduce-scatter.2.cloned.1.call-done = bf16[15,8,1440]{2,1,0:T(8,128)(2,1)} async-done(((bf16[480,8,1440]{2,1,0:T(8,128)(2,1)}), bf16[15,8,1440]{2,1,0:T(8,128)(2,1)}) %reduce-scatter.2.cloned.1.call-update) | async-done | bytes 345616 | tf_op jit(solution)/shard_map/reduce_scatter | solution.py:101
  592.2 3.0 reshape.141
  595.3 2.6 copy.110
  599.5 3.0 collective-permute-start.4
  602.5 1.3 collective-permute-start.5
  604.7 1.8 collective-permute-done.4
  606.5 4.6 collective-permute-done.5
  611.1 1.3 maximum_convert_fusion.2
  614.2 2.7 collective-permute-start.6
  616.9 1.5 collective-permute-start.7
  618.4 2.9 collective-permute-done.6
  621.4 3.8 collective-permute-done.7
  626.3 1.5 copy.112
  627.8 2.0 reshape.153
  629.8 19.2 %all_to_all.56 = bf16[8,2,10800]{2,1,0:T(2,128)(2,1)S(1)} all-to-all(bf16[8,2,10800]{2,1,0:T(2,128)(2,1)S(1)} %reshape.153), channel_id=1, replica_groups=mesh['space'=32,'tm'=8] {'tm'}, dimensions={0} | all-to-all | bytes 691200 | tf_op jit(solution)/shard_map/all_to_all | solution.py:41
  649.0 1.8 reshape.154
  652.8 12.3 %all_to_all.57 = bf16[8,240,90]{2,0,1:T(8,128)(2,1)S(1)} all-to-all(bf16[8,240,90]{2,0,1:T(8,128)(2,1)S(1)} %copy.116), channel_id=1, replica_groups=mesh['space'=32,'tm'=8] {'tm'}, dimensions={1} | all-to-all | bytes 691200 | tf_op jit(solution)/shard_map/all_to_all | solution.py:46
  667.8 81.2 %all-reduce = (f32[8]{0:T(128)S(1)}, f32[8]{0:T(128)S(1)}) all-reduce(f32[8]{0:T(128)S(1)} %get-tuple-element.31, f32[8]{0:T(128)S(1)} %get-tuple-element.7), channel_id=1, replica_groups=mesh['space'=32,'tm'=8] {'space','tm'}, use_global_device_ids=true, to_apply=%region_1.2 | all-reduce | flops 16 | bytes 128 | tf_op jit(solution)/shard_map/psum | solution.py:116
  749.0 1.5 multiply_reduce_fusion
  750.5 73.2 %psum.23 = f32[8]{0:T(128)S(1)} all-reduce(f32[8]{0:T(128)S(1)} %get-tuple-element.5), channel_id=1, replica_groups=mesh['space'=32,'tm'=8] {'space','tm'}, use_global_device_ids=true, to_apply=%region_6.7 | all-reduce | flops 8 | bytes 64 | tf_op jit(solution)/shard_map/psum | solution.py:122
  823.8 2.5 multiply_add_fusion
  (73 shorter events, 24.1 us)
Async XLA Ops:
  7.2 329.7 %copy-start = (bf16[1,8,64,1440]{3,2,1,0:T(8,128)(2,1)S(1)}, bf16[1,8,64,1440]{3,2,1,0:T(8,128)(2,1)}, u32[]{:S(2)}) copy-start(bf16[1,8,64,1440]{3,2,1,0:T(8,128)(2,1)} %param.14) | copy-start | bytes 4423684
  7.2 302.4 %all-gather.2.cloned.1.call-start = ((), (), s32[]{:S(2)}) async-start(), calls=%async_computation.5 | async-start | bytes 30412800 | tf_op jit(solution)/shard_map/all_gather | solution.py:84
  44.4 1.5 copy-start.11
  47.9 9.9 %collective-permute-start = (bf16[8,30,720]{2,0,1:T(8,128)(2,1)}, bf16[8,30,720]{2,0,1:T(8,128)(2,1)}, u32[]{:S(2)}, u32[]{:S(2)}) collective-permute-start(bf16[8,30,720]{2,0,1:T(8,128)(2,1)} %multiply_convert_fusion.6), channel_id=1, source_target_pairs={{0,8},{8,16},{16,24},{24,32},{32,40},{40,48},{48,56},{56,64},{64,7... | collective-permute-start | bytes 1036808 | tf_op jit(solution)/shard_map/ppermute | solution.py:28
  51.3 11.0 %collective-permute-start.1 = (bf16[8,30,720]{2,0,1:T(8,128)(2,1)}, bf16[8,30,720]{2,0,1:T(8,128)(2,1)}, u32[]{:S(2)}, u32[]{:S(2)}) collective-permute-start(bf16[8,30,720]{2,0,1:T(8,128)(2,1)} %multiply_convert_fusion.6), channel_id=1, source_target_pairs={{8,0},{16,8},{24,16},{32,24},{40,32},{48,40},{56,48},{64,56},{72,6... | collective-permute-start | bytes 1036808 | tf_op jit(solution)/shard_map/ppermute | solution.py:30
  63.6 1.1 copy-start.3
  64.7 2.0 copy-start.6
  65.8 0.9 copy-start.2
  67.5 11.8 %collective-permute-start.2 = (bf16[8,30,720]{2,0,1:T(8,128)(2,1)}, bf16[8,30,720]{2,0,1:T(8,128)(2,1)}, u32[]{:S(2)}, u32[]{:S(2)}) collective-permute-start(bf16[8,30,720]{2,0,1:T(8,128)(2,1)} %fusion.47), channel_id=1, source_target_pairs={{0,8},{8,16},{16,24},{24,32},{32,40},{40,48},{48,56},{56,64},{64,7... | collective-permute-start | bytes 1036808 | tf_op jit(solution)/shard_map/ppermute | solution.py:28
  70.7 9.8 %collective-permute-start.3 = (bf16[8,30,720]{2,0,1:T(8,128)(2,1)}, bf16[8,30,720]{2,0,1:T(8,128)(2,1)}, u32[]{:S(2)}, u32[]{:S(2)}) collective-permute-start(bf16[8,30,720]{2,0,1:T(8,128)(2,1)} %fusion.47), channel_id=1, source_target_pairs={{8,0},{16,8},{24,16},{32,24},{40,32},{48,40},{56,48},{64,56},{72,6... | collective-permute-start | bytes 1036808 | tf_op jit(solution)/shard_map/ppermute | solution.py:30
  92.3 1.4 copy-start.12
  93.5 498.7 %reduce-scatter.2.cloned.1.call-start = ((), (), s32[]{:S(2)}) async-start(), calls=%async_computation.6 | async-start | bytes 12165120 | tf_op jit(solution)/shard_map/reduce_scatter | solution.py:101
  309.6 27.3 %copy-start.13 = (f32[1,1,64]{2,1,0:T(1,128)S(1)}, f32[1,1,64]{2,1,0:T(1,128)}, u32[]{:S(2)}) copy-start(f32[1,1,64]{2,1,0:T(1,128)} %param.15) | copy-start | bytes 772
  599.5 7.0 collective-permute-start.4
  602.5 8.6 %collective-permute-start.5 = (bf16[8,30,720]{2,0,1:T(8,128)(2,1)}, bf16[8,30,720]{2,0,1:T(8,128)(2,1)}, u32[]{:S(2)}, u32[]{:S(2)}) collective-permute-start(bf16[8,30,720]{2,0,1:T(8,128)(2,1)} %multiply_convert_fusion.3), channel_id=1, source_target_pairs={{8,0},{16,8},{24,16},{32,24},{40,32},{48,40},{56,48},{64,56},{72,6... | collective-permute-start | bytes 1036808 | tf_op jit(solution)/shard_map/ppermute | solution.py:30
  604.7 7.7 copy-start.4
  612.5 1.1 copy-start.5
  614.2 7.1 collective-permute-start.6
  616.9 8.3 collective-permute-start.7
  649.0 2.9 copy-start.10
  665.1 1.1 copy-start.7
  665.5 1.2 copy-start.8
  750.5 75.8 %copy-start.9 = (f32[8,30,720]{2,0,1:T(8,128)}, f32[8,30,720]{2,0,1:T(8,128)S(1)}, u32[]{:S(2)}) copy-start(f32[8,30,720]{2,0,1:T(8,128)S(1)} %get-tuple-element.6) | copy-start | bytes 2073604
  823.8 2.6 copy-start.1
Sparse Core Ops, SparseCore 0:
  93.6 215.9 all-gather.1
  362.4 229.8 reduce-scatter.1
where the time goes:
time: 841 us; the launch traced here: 833 us
  waiting for transfers between devices  468 us (56%)
  blocking collectives  212 us (25%)
  local copies, waits for them, and re-layouts  62.5 us (7%)
  matrix products  33.5 us (4%)
  other arithmetic  25.1 us (3%)
  starting transfers between devices  18 us (2%)
  between operations  14.6 us (2%)
    reduce_scatter x1, waiting for transfers between devices, local(): lax.psum_scatter(jnp.einsum('bj,bkx->jkx', selector, gradient, preferred_...  230 us
    all_gather x1, waiting for transfers between devices, local(): segment = lax.all_gather(tiled, 'space', axis=2, tiled=True)  216 us
    psum x1, blocking collectives, local(): lax.psum((jnp.sum(residual * residual, axis=(1, 2)), jnp.sum(direction *...  81.2 us
    psum x1, blocking collectives, local(): lax.psum(jnp.sum(residual_next * residual_next, axis=(1, 2)), ('space', '...  73.2 us
    all_to_all x2, blocking collectives, temporal(): lax.all_to_all(field.astype(jnp.bfloat16), 'tm', split_axis=2, concat_axi...  33.1 us
    dot_general x1, matrix products, local(): jnp.einsum('bj,ktjc->bktc', selector, segment, preferred_element_type=jnp...  26.4 us
    all_to_all x2, blocking collectives, temporal(): lax.all_to_all(for_sending(combined), 'tm', split_axis=1, concat_axis=2,...  24.5 us
    convert_element_type x1, local copies, waits for them, and re-layouts, local(): jnp.einsum('bj,bkx->jkx', selector, gradient, preferred_element_type=jnp....  20.4 us
  transfers between devices with their start and end apart: 10, of which 9 were waited for; matrix products, arithmetic and copies ran while one was open for 1% of the time, Pallas kernels for 0%

commit v1 on v0

--- a/solution.py
+++ b/solution.py
@@ -7,6 +7,12 @@
 TC = 48
 NB = 8
 DIFF = 2
+
+
+def tiled_gather(x, axis, dim):
+    devices = lax.axis_size(axis)
+    repeats = [devices if d == dim else 1 for d in range(x.ndim)]
+    return lax.all_to_all(jnp.tile(x, repeats), axis, split_axis=dim, concat_axis=dim, tiled=True)
 
 
 def for_sending(value):
@@ -81,7 +87,7 @@
     spread = diffuse(mixed, diffusivity)
     tiled = spread.astype(jnp.bfloat16).reshape(samples, window, tiles_here, TC)
     empty_blocks = jnp.zeros((blocks_here, samples, window * TC), jnp.float32)
-    segment = lax.all_gather(tiled, "space", axis=2, tiled=True)
+    segment = tiled_gather(tiled, "space", 2)
     count_tiles = segment.shape[2]
     selector = (entries[:, None] == jnp.arange(count_tiles)[None, :]).astype(jnp.bfloat16)
     picked = jnp.einsum("bj,ktjc->bktc", selector, segment, preferred_element_type=jnp.float32)

time: 841 us -> 1020 us (1.21)
  local copies, waits for them, and re-layouts: 62.5 us -> 188 us
  waiting for transfers between devices: 468 us -> 499 us
  starting transfers between devices: 18 us -> 32.7 us
    all_to_all x0 -> x1, waiting for transfers between devices: none -> 236 us  [tiled_gather(): lax.all_to_all(jnp.tile(x, repeats), axis, split_axis=dim, concat_axis=di...]
    all_gather x1 -> x0, waiting for transfers between devices: 216 us -> none  [local(): segment = lax.all_gather(tiled, 'space', axis=2, tiled=True)]
    unnamed x32 -> x28, local copies, waits for them, and re-layouts: 12.3 us -> 106 us
    another operation x0 -> x2, local copies, waits for them, and re-layouts: none -> 30.3 us  [tiled_gather(): jnp.tile(x, repeats)]
    all_to_all x0 -> x1, starting transfers between devices: none -> 15 us  [tiled_gather(): lax.all_to_all(jnp.tile(x, repeats), axis, split_axis=dim, concat_axis=di...]
    reduce_scatter x1, waiting for transfers between devices: 230 us -> 244 us  [local(): lax.psum_scatter(jnp.einsum('bj,bkx->jkx', selector, gradient, preferred_...]
  transfers between devices with their start and end apart: 10 -> 10, of which waited for: 9 -> 8; matrix products, arithmetic and copies ran while one was open for 1% -> 1% of each run, Pallas kernels for 0% -> 0%
where the time goes in v1:
time: 1020 us; the launch traced here: 1010 us
  waiting for transfers between devices  499 us (49%)
  blocking collectives  212 us (21%)
  local copies, waits for them, and re-layouts  188 us (18%)
  matrix products  34.6 us (3%)
  starting transfers between devices  32.7 us (3%)
  other arithmetic  29.5 us (3%)
  between operations  14.6 us (1%)
    reduce_scatter x1, waiting for transfers between devices, local(): lax.psum_scatter(jnp.einsum('bj,bkx->jkx', selector, gradient, preferred_...  244 us
    all_to_all x1, waiting for transfers between devices, tiled_gather(): lax.all_to_all(jnp.tile(x, repeats), axis, split_axis=dim, concat_axis=di...  236 us
    unnamed x28, local copies, waits for them, and re-layouts  106 us
    psum x1, blocking collectives, local(): lax.psum((jnp.sum(residual * residual, axis=(1, 2)), jnp.sum(direction *...  81.2 us
    psum x1, blocking collectives, local(): lax.psum(jnp.sum(residual_next * residual_next, axis=(1, 2)), ('space', '...  73.2 us
    all_to_all x2, blocking collectives, temporal(): lax.all_to_all(field.astype(jnp.bfloat16), 'tm', split_axis=2, concat_axi...  33.2 us
    another operation x2, local copies, waits for them, and re-layouts, tiled_gather(): jnp.tile(x, repeats)  30.3 us
    dot_general x1, matrix products, local(): jnp.einsum('bj,ktjc->bktc', selector, segment, preferred_element_type=jnp...  26.6 us
  transfers between devices with their start and end apart: 10, of which 8 were waited for; matrix products, arithmetic and copies ran while one was open for 1% of the time, Pallas kernels for 0%

profile of v1, /device:TPU:1, one launch (start us, length us, event | category | flops | bytes accessed | tf_op | source)
XLA Modules:
  0.0 1010.4 jit_solution(9679598313135398603)
XLA Ops:
  8.5 1.5 copy.97
  10.0 2.0 reshape.172
  12.0 14.0 %all_to_all.59 = bf16[8,2,10800]{2,1,0:T(2,128)(2,1)} all-to-all(bf16[8,2,10800]{2,1,0:T(2,128)(2,1)S(1)} %reshape.172), channel_id=1, replica_groups=mesh['space'=32,'tm'=8] {'tm'}, dimensions={0} | all-to-all | bytes 691200 | tf_op jit(solution)/shard_map/all_to_all | solution.py:47
  25.9 3.1 reshape.173
  30.2 1.6 fusion.12
  32.1 12.3 %all_to_all.60 = bf16[8,240,90]{2,0,1:T(8,128)(2,1)S(1)} all-to-all(bf16[8,240,90]{2,0,1:T(8,128)(2,1)S(1)} %copy.100), channel_id=1, replica_groups=mesh['space'=32,'tm'=8] {'tm'}, dimensions={1} | all-to-all | bytes 691200 | tf_op jit(solution)/shard_map/all_to_all | solution.py:52
  45.9 1.9 multiply_convert_fusion.6
  47.8 3.4 collective-permute-start
  54.8 2.8 collective-permute-done
  57.7 4.6 collective-permute-done.1
  67.5 3.1 collective-permute-start.2
  70.6 1.5 collective-permute-start.3
  73.4 2.7 reshape.158
  76.1 3.1 reshape.149
  84.3 3.1 reshape.151
  87.3 4.9 fusion.5
  92.3 9.9 tile.8
  102.2 20.4 %copy.145 = bf16[8,30,480,48]{3,0,1,2:T(8,128)(2,1)} copy(bf16[8,30,480,48]{3,0,2,1:T(8,128)(2,1)} %bitcast.145) | data formatting | bytes 22118400 | tf_op jit(solution)/shard_map/tile | solution.py:15
  122.5 50.2 %reshape.174 = bf16[32,2,86400]{2,1,0:T(2,128)(2,1)} reshape(bf16[480,30,8,48]{3,2,1,0:T(8,128)(2,1)} %bitcast.146) | data formatting | bytes 22118400
  172.8 15.0 %all-to-all-start.2 = ((bf16[32,2,86400]{2,1,0:T(2,128)(2,1)}), bf16[32,2,86400]{2,1,0:T(2,128)(2,1)}, u32[]{:S(2)}, u32[]{:S(2)}) async-start(bf16[32,2,86400]{2,1,0:T(2,128)(2,1)} %reshape.174), calls=%async_computation.2 | async-start | bytes 22118400 | tf_op jit(solution)/shard_map/all_to_all | solution.py:15
  187.9 235.7 %all-to-all-done.2 = bf16[32,2,86400]{2,1,0:T(2,128)(2,1)} async-done(((bf16[32,2,86400]{2,1,0:T(2,128)(2,1)}), bf16[32,2,86400]{2,1,0:T(2,128)(2,1)}, u32[]{:S(2)}, u32[]{:S(2)}) %all-to-all-start.2) | async-done | bytes 11059232 | tf_op jit(solution)/shard_map/all_to_all | solution.py:15
  423.5 42.2 %reshape.175 = bf16[480,30,8,48]{3,2,1,0:T(8,128)(2,1)} reshape(bf16[32,2,86400]{2,1,0:T(2,128)(2,1)} %all-to-all-done.2) | data formatting | bytes 22118400
  465.7 26.6 %fusion.9 = bf16[8,8,30,48]{3,0,2,1:T(8,128)(2,1)S(1)} fusion(bf16[8,30,480,48]{3,0,1,2:T(8,128)(2,1)} %bitcast.147, s32[8]{0:T(128)S(1)} %bitcast.161), kind=kOutput, calls=%fused_computation.14 | convolution fusion | flops 88569600 | bytes 11243552 | tf_op jit(solution)/shard_map/bj,ktjc->bktc/dot_general | solution.py:93
  494.4 3.7 convolution_convert_fusion
  498.1 20.4 %copy.111 = bf16[480,8,1440]{2,1,0:T(8,128)(2,1)} copy(bf16[480,8,1440]{2,0,1:T(8,128)(2,1)S(1)} %convolution_convert_fusion) | data formatting | bytes 22118400 | tf_op jit(solution)/shard_map/convert_element_type | solution.py:108
  518.5 243.8 %reduce-scatter.2.cloned.1.call-done = bf16[15,8,1440]{2,1,0:T(8,128)(2,1)} async-done(((bf16[480,8,1440]{2,1,0:T(8,128)(2,1)}), bf16[15,8,1440]{2,1,0:T(8,128)(2,1)}) %reduce-scatter.2.cloned.1.call-update) | async-done | bytes 345616 | tf_op jit(solution)/shard_map/reduce_scatter | solution.py:107
  762.4 3.0 reshape.162
  765.4 2.6 copy.112
  768.1 1.7 reshape.154
  769.7 1.9 multiply_convert_fusion.3
  771.6 3.0 collective-permute-start.4
  775.9 1.7 reshape.155
  778.8 4.4 collective-permute-done.5
  786.8 2.6 collective-permute-start.6
  789.5 1.5 collective-permute-start.7
  790.9 2.9 collective-permute-done.6
  793.9 3.8 collective-permute-done.7
  798.7 1.5 copy.114
  800.3 2.0 reshape.176
  802.2 19.2 %all_to_all.61 = bf16[8,2,10800]{2,1,0:T(2,128)(2,1)} all-to-all(bf16[8,2,10800]{2,1,0:T(2,128)(2,1)S(1)} %reshape.176), channel_id=1, replica_groups=mesh['space'=32,'tm'=8] {'tm'}, dimensions={0} | all-to-all | bytes 691200 | tf_op jit(solution)/shard_map/all_to_all | solution.py:47
  821.5 3.1 reshape.177
  825.7 1.6 fusion.13
  827.6 12.3 %all_to_all.62 = bf16[8,240,90]{2,0,1:T(8,128)(2,1)S(1)} all-to-all(bf16[8,240,90]{2,0,1:T(8,128)(2,1)S(1)} %copy.118), channel_id=1, replica_groups=mesh['space'=32,'tm'=8] {'tm'}, dimensions={1} | all-to-all | bytes 691200 | tf_op jit(solution)/shard_map/all_to_all | solution.py:52
  841.5 2.5 multiply_reduce_fusion.1
  844.0 81.2 %all-reduce = (f32[8]{0:T(128)S(1)}, f32[8]{0:T(128)S(1)}) all-reduce(f32[8]{0:T(128)S(1)} %get-tuple-element.31, f32[8]{0:T(128)S(1)} %get-tuple-element.7), channel_id=1, replica_groups=mesh['space'=32,'tm'=8] {'space','tm'}, use_global_device_ids=true, to_apply=%region_1.2 | all-reduce | flops 16 | bytes 128 | tf_op jit(solution)/shard_map/psum | solution.py:122
  925.2 2.3 multiply_reduce_fusion
  927.5 73.2 %psum.23 = f32[8]{0:T(128)S(1)} all-reduce(f32[8]{0:T(128)S(1)} %get-tuple-element.5), channel_id=1, replica_groups=mesh['space'=32,'tm'=8] {'space','tm'}, use_global_device_ids=true, to_apply=%region_6.7 | all-reduce | flops 8 | bytes 64 | tf_op jit(solution)/shard_map/psum | solution.py:128
  1000.7 2.6 multiply_add_fusion
  (69 shorter events, 31.6 us)
Async XLA Ops:
  7.2 486.0 %copy-start = (bf16[1,8,64,1440]{3,2,1,0:T(8,128)(2,1)S(1)}, bf16[1,8,64,1440]{3,2,1,0:T(8,128)(2,1)}, u32[]{:S(2)}) copy-start(bf16[1,8,64,1440]{3,2,1,0:T(8,128)(2,1)} %param.14) | copy-start | bytes 4423684
  44.4 1.5 copy-start.8
  47.8 9.9 collective-permute-start
  51.2 11.0 %collective-permute-start.1 = (bf16[8,30,720]{2,0,1:T(8,128)(2,1)}, bf16[8,30,720]{2,0,1:T(8,128)(2,1)}, u32[]{:S(2)}, u32[]{:S(2)}) collective-permute-start(bf16[8,30,720]{2,0,1:T(8,128)(2,1)} %multiply_convert_fusion.6), channel_id=1, source_target_pairs={{8,0},{16,8},{24,16},{32,24},{40,32},{48,40},{56,48},{64,56},{72,6... | collective-permute-start | bytes 1036808 | tf_op jit(solution)/shard_map/ppermute | solution.py:36
  63.5 1.1 copy-start.3
  64.6 2.0 copy-start.5
  65.8 0.9 copy-start.2
  67.5 11.8 %collective-permute-start.2 = (bf16[8,30,720]{2,0,1:T(8,128)(2,1)}, bf16[8,30,720]{2,0,1:T(8,128)(2,1)}, u32[]{:S(2)}, u32[]{:S(2)}) collective-permute-start(bf16[8,30,720]{2,0,1:T(8,128)(2,1)} %fusion.47), channel_id=1, source_target_pairs={{0,8},{8,16},{16,24},{24,32},{32,40},{40,48},{48,56},{56,64},{64,7... | collective-permute-start | bytes 1036808 | tf_op jit(solution)/shard_map/ppermute | solution.py:34
  70.6 9.8 collective-permute-start.3
  172.8 15.1 %copy-start.9 = (s32[1,8]{1,0:T(1,128)S(1)}, s32[1,8]{1,0:T(1,128)}, u32[]{:S(2)}) copy-start(s32[1,8]{1,0:T(1,128)} %param.13) | copy-start | bytes 100
  172.8 250.7 %all-to-all-start.2 = ((bf16[32,2,86400]{2,1,0:T(2,128)(2,1)}), bf16[32,2,86400]{2,1,0:T(2,128)(2,1)}, u32[]{:S(2)}, u32[]{:S(2)}) async-start(bf16[32,2,86400]{2,1,0:T(2,128)(2,1)} %reshape.174), calls=%async_computation.2 | async-start | bytes 22118400 | tf_op jit(solution)/shard_map/all_to_all | solution.py:15
  187.8 574.6 %reduce-scatter.2.cloned.1.call-start = ((), (), s32[]{:S(2)}) async-start(), calls=%async_computation.6 | async-start | bytes 12165120 | tf_op jit(solution)/shard_map/reduce_scatter | solution.py:107
  465.7 27.5 %copy-start.10 = (f32[1,1,64]{2,1,0:T(1,128)S(1)}, f32[1,1,64]{2,1,0:T(1,128)}, u32[]{:S(2)}) copy-start(f32[1,1,64]{2,1,0:T(1,128)} %param.15) | copy-start | bytes 772
  771.6 7.1 collective-permute-start.4
  774.6 8.6 collective-permute-start.5
  784.5 1.1 copy-start.4
  785.6 1.1 copy-start.1
  786.8 7.0 collective-permute-start.6
  789.5 8.3 collective-permute-start.7
  839.9 1.5 copy-start.6
  841.5 83.8 %copy-start.7 = (f32[8,30,720]{2,0,1:T(8,128)S(1)}, f32[8,30,720]{2,0,1:T(8,128)}, u32[]{:S(2)}) copy-start(f32[8,30,720]{2,0,1:T(8,128)} %param.9) | copy-start | bytes 2073604
Sparse Core Ops, SparseCore 0:
  518.7 243.6 reduce-scatter.1
